TPU v7x, 128 devices: a whole 4x4x4 slice. The times are simulated.
128 devices in a mesh: img: 4 (over y_lo, core), tile: 32 (over x, y_hi, z).
Axes of the slice: x: 4, y: 4 (y_hi: 2, y_lo: 2; y = y_hi * 2 + y_lo), z: 4, core: 2. Of those that a mesh axis runs over, the one named last changes fastest.
Arguments:
- tiles: bfloat16 [32768, 1152], P(('img', 'tile')), may hold values from -6 to 6
- tile_image: int32 [128], P(('img', 'tile')), may hold values from 0 to 1
- guide: bfloat16 [8, 512, 1152], P('img', 'tile'), may hold values from -160 to 160
- gain: float32 [1152], replicated, may hold values from 0.5 to 1.5
- w_query: bfloat16 [1152, 1152], replicated, may hold values from -0.1875 to 0.1875
- w_key: bfloat16 [1152, 1152], replicated, may hold values from -0.1875 to 0.1875
- w_value: bfloat16 [1152, 1152], replicated, may hold values from -0.1875 to 0.1875
- w_out: bfloat16 [1152, 1152], replicated, may hold values from -0.1875 to 0.1875
- grad_out: bfloat16 [32768, 1152], P(('img', 'tile')), may hold values from -24 to 24
Outputs:
- grad_tiles: bfloat16 [32768, 1152], P(('img', 'tile'))
- grad_guide: bfloat16 [8, 512, 1152], P('img', 'tile')
- grad_weights: float32 [4, 1152, 1152], P(None, ('img', 'tile'))
- grad_gain: float32 [1152], replicated
Inputs may be any that keep to these rules, and one draw needn't show every extreme that they name: `tile_image`: image of each tile within its own img group of 2 images.
All inputs are finite; a program needn't handle non-finite values.
Results may differ from a plain program's by a relative error of at most 0.034.
The roundings to bfloat16 on the way count: a program that leaves them out, or rounds other values in their place, can miss the bound.
Values may be sent and summed in bfloat16 or wider, within the bound.
No kernel may reach another device: no remote copies, remote signals or barrier semaphores. Data moves between devices by JAX's collectives and lax.ppermute only.
A program may use at most 128 MiB of HBM per device.

v0:
```python
import jax
import jax.numpy as jnp
from jax import lax
from jax.sharding import PartitionSpec as P

HEADS = 16
TILE = 256


def laid_out(blocks, dim):
    lengths = list(blocks.shape[1:])
    lengths[dim] *= blocks.shape[0]
    return jnp.moveaxis(blocks, 0, dim).reshape(lengths)


def copy_for_each(x, axis):
    copies = jnp.broadcast_to(x, (lax.axis_size(axis), *x.shape))
    return lax.all_to_all(copies, axis, split_axis=0, concat_axis=0, tiled=True)


def gather_directly(x, axis, dim):
    return laid_out(copy_for_each(x, axis), dim)


def in_one_piece(arrays, axis, dim, along):
    ends, at = ([], 0)
    for a in arrays[:-1]:
        at += a.shape[along]
        ends.append(at)
    both = jnp.concatenate(arrays, axis=along)
    return tuple(
        jnp.split(lax.psum_scatter(both, axis, scatter_dimension=dim, tiled=True), ends, axis=along)
    )


def tile_pass(q_tile, k_img, v_img, d_tile):
    width = q_tile.shape[1]
    head_size = width // HEADS
    scale = head_size ** (-0.5)
    rows = q_tile.shape[0]
    keyrows = k_img.shape[0]
    qh = q_tile.reshape(rows, HEADS, head_size)
    kh = k_img.reshape(keyrows, HEADS, head_size)
    vh = v_img.reshape(keyrows, HEADS, head_size)
    dh = d_tile.reshape(rows, HEADS, head_size)
    scores = jnp.einsum("qhd,khd->hqk", qh, kh, preferred_element_type=jnp.float32) * scale
    top = jnp.max(scores, axis=-1, keepdims=True)
    expo = jnp.exp(scores - top)
    probs = expo / jnp.sum(expo, axis=-1, keepdims=True)
    pb = probs.astype(jnp.bfloat16)
    outv = jnp.einsum("hqk,khd->qhd", pb, vh, preferred_element_type=jnp.float32).astype(
        jnp.bfloat16
    )
    dprob = jnp.einsum("qhd,khd->hqk", dh, vh, preferred_element_type=jnp.float32)
    delta = jnp.sum(probs * dprob, axis=-1, keepdims=True)
    dscore = (probs * (dprob - delta) * scale).astype(jnp.bfloat16)
    dq = jnp.einsum("hqk,khd->qhd", dscore, kh, preferred_element_type=jnp.float32).astype(
        jnp.bfloat16
    )
    dk = jnp.einsum("hqk,qhd->khd", dscore, qh, preferred_element_type=jnp.float32).reshape(
        keyrows, width
    )
    dv = jnp.einsum("hqk,qhd->khd", pb, dh, preferred_element_type=jnp.float32).reshape(
        keyrows, width
    )
    return (outv.reshape(rows, width), dq.reshape(rows, width), dk, dv)


def project(rows_in, weight):
    flat = rows_in.reshape(-1, rows_in.shape[-1])
    result = jnp.dot(flat, weight, preferred_element_type=jnp.float32).astype(jnp.bfloat16)
    return result.reshape(rows_in.shape)


def on_device(tiles, tile_image, guide, gain, w_query, w_key, w_value, w_out, grad_out):
    width = tiles.shape[1]
    tile_count = tile_image.shape[0]
    xf = tiles.astype(jnp.float32)
    rstd = lax.rsqrt(jnp.mean(xf * xf, axis=-1, keepdims=True) + 1e-06)
    normed = xf * rstd
    hidden = (normed * gain).astype(jnp.bfloat16)
    query = jnp.dot(hidden, w_query, preferred_element_type=jnp.float32).astype(jnp.bfloat16)
    whole = gather_directly(guide, "tile", 1)
    keys = project(whole, w_key)
    values = project(whole, w_value)
    dout = jnp.einsum("td,ed->te", grad_out, w_out, preferred_element_type=jnp.float32).astype(
        jnp.bfloat16
    )

    def step(carry, item):
        dk_acc, dv_acc = carry
        q_tile, d_tile, image = item
        k_img = lax.dynamic_index_in_dim(keys, image, 0, keepdims=False)
        v_img = lax.dynamic_index_in_dim(values, image, 0, keepdims=False)
        outv, dq, dk, dv = tile_pass(q_tile, k_img, v_img, d_tile)
        old_k = lax.dynamic_index_in_dim(dk_acc, image, 0, keepdims=False)
        old_v = lax.dynamic_index_in_dim(dv_acc, image, 0, keepdims=False)
        dk_acc = lax.dynamic_update_index_in_dim(dk_acc, old_k + dk, image, 0)
        dv_acc = lax.dynamic_update_index_in_dim(dv_acc, old_v + dv, image, 0)
        return ((dk_acc, dv_acc), (outv, dq))

    start = (jnp.zeros(keys.shape, jnp.float32), jnp.zeros(keys.shape, jnp.float32))
    items = (
        query.reshape(tile_count, TILE, width),
        dout.reshape(tile_count, TILE, width),
        tile_image,
    )
    (dk_all, dv_all), (outs, dqs) = lax.scan(step, start, items)
    outv = outs.reshape(-1, width)
    dq = dqs.reshape(-1, width)
    dk_mine, dv_mine = tuple(
        (
            part.astype(jnp.float32)
            for part in in_one_piece(
                (dk_all.astype(jnp.bfloat16), dv_all.astype(jnp.bfloat16)), "tile", 1, 0
            )
        )
    )
    dkb = dk_mine.astype(jnp.bfloat16).reshape(-1, width)
    dvb = dv_mine.astype(jnp.bfloat16).reshape(-1, width)
    flat = guide.reshape(-1, width)
    grad_guide = (
        (
            jnp.einsum("ge,de->gd", dkb, w_key, preferred_element_type=jnp.float32)
            + jnp.einsum("ge,de->gd", dvb, w_value, preferred_element_type=jnp.float32)
        )
        .astype(jnp.bfloat16)
        .reshape(guide.shape)
    )
    dh = jnp.einsum("te,de->td", dq, w_query, preferred_element_type=jnp.float32)
    grad_gain = lax.psum(jnp.sum(dh * normed, axis=0), ("img", "tile"))
    dn = dh * gain
    grad_tiles = (rstd * (dn - normed * jnp.mean(dn * normed, axis=-1, keepdims=True))).astype(
        jnp.bfloat16
    )
    stacked = jnp.stack(
        [
            jnp.einsum("td,te->de", hidden, dq, preferred_element_type=jnp.float32),
            jnp.einsum("td,te->de", flat, dkb, preferred_element_type=jnp.float32),
            jnp.einsum("td,te->de", flat, dvb, preferred_element_type=jnp.float32),
            jnp.einsum("td,te->de", outv, grad_out, preferred_element_type=jnp.float32),
        ]
    )
    grad_weights = lax.psum_scatter(stacked, ("img", "tile"), scatter_dimension=1, tiled=True)
    return (grad_tiles, grad_guide, grad_weights, grad_gain)


def solution(mesh):
    return jax.shard_map(
        on_device,
        mesh=mesh,
        in_specs=(
            P(("img", "tile"), None),
            P(("img", "tile")),
            P("img", "tile", None),
            P(),
            P(),
            P(),
            P(),
            P(),
            P(("img", "tile"), None),
        ),
        out_specs=(
            P(("img", "tile"), None),
            P("img", "tile", None),
            P(None, ("img", "tile"), None),
            P(),
        ),
        check_vma=False,
    )
```

profile of v0, /device:TPU:2, one launch (start us, length us, event | category | flops | bytes accessed | tf_op | source)
XLA Modules:
  0.0 635.1 jit_solution(12756017101563433656)
XLA Ops:
  7.2 0.0 copy-start
  7.2 2.6 broadcast_in_dim.27
  9.8 11.1 %all-to-all-start = ((bf16[32,2,16,1152]{3,2,1,0:T(8,128)(2,1)}), bf16[32,2,16,1152]{3,2,1,0:T(8,128)(2,1)}, u32[]{:S(2)}, u32[]{:S(2)}) async-start(bf16[32,2,16,1152]{3,2,1,0:T(8,128)(2,1)} %broadcast_in_dim.27), calls=%async_computation | async-start | bytes 4718592 | tf_op jit(solution)/shard_map/all_to_all | solution.py:18
  20.9 0.0 reduce-scatter.2.cloned.1.call-start
  21.6 0.0 copy-start.1
  21.6 0.0 copy-start.10
  21.6 3.8 convolution_convert_fusion.2
  25.5 2.1 copy.36
  27.6 0.0 copy-done.1
  27.6 0.2 fusion.36
  27.8 0.0 copy-done.10
  27.8 3.6 convolution_convert_fusion.3
  31.5 2.1 copy.35
  33.6 17.4 %all-to-all-done = bf16[32,2,16,1152]{3,2,1,0:T(8,128)(2,1)} async-done(((bf16[32,2,16,1152]{3,2,1,0:T(8,128)(2,1)}), bf16[32,2,16,1152]{3,2,1,0:T(8,128)(2,1)}, u32[]{:S(2)}, u32[]{:S(2)}) %all-to-all-start) | async-done | bytes 2359328 | tf_op jit(solution)/shard_map/all_to_all | solution.py:18
  51.0 1.8 copy.33
  52.9 0.0 copy-start.6
  52.9 0.0 copy-done
  52.9 3.9 convolution_convert_fusion.1
  56.8 0.0 copy-done.6
  56.8 1.1 constant_dynamic-slice_fusion.1
  57.9 2.4 copy.34
  60.3 7.4 %fusion.47 = (f32[16,256]{1,0:T(8,128)S(1)}, f32[16,256,512]{2,1,0:T(8,128)}) fusion(bf16[256,16,72]{0,2,1:T(8,128)(2,1)} %bitcast.91, bf16[512,16,72]{0,2,1:T(8,128)(2,1)} %bitcast.83), kind=kOutput, calls=%fused_computation.57 | convolution fusion | flops 308281856 | bytes 10174464 | tf_op jit(solution)/shard_map/while/body/eval_jaxpr/sub | solution.py:48
  67.7 5.5 fusion.18
  73.2 2.4 copy.39
  75.6 6.0 convolution_convert_fusion
  81.5 0.0 copy-start.3
  81.5 1.6 broadcast.37.clone
  83.1 0.1 copy-done.3
  83.2 1.6 constant_dynamic-update-slice_fusion
  84.8 2.4 copy.37
  87.2 6.0 fusion.48
  93.2 34.4 %fusion.10 = bf16[16,72,512]{2,1,0:T(8,128)(2,1)} fusion(bf16[256,16,72]{0,2,1:T(8,128)(2,1)} %bitcast.92, f32[16,256,512]{2,1,0:T(8,128)} %fusion.48, f32[16,256,512]{2,1,0:T(8,128)} %get-tuple-element.47, f32[16,256]{1,0:T(8,128)S(1)} %get-tuple-element.46), kind=kOutput, calls=%fused_computation.16 | convolution fusion | flops 316674560 | bytes 18563072 | tf_op jit(solution)/shard_map/while/body/eval_jaxpr/hqk,qhd->khd/dot_general | solution.py:60
  127.6 2.4 copy.38
  130.0 0.2 broadcast.37
  130.1 1.1 copy-done.4
  131.2 0.2 constant_dynamic-update-slice_fusion.1
  131.4 4.3 pad_maximum_fusion.1
  135.7 0.0 reduce-scatter.2.cloned.1.call-update
  135.8 0.0 all-reduce.3.cloned.1.call-start
  135.8 0.0 copy-start.9
  135.8 5.3 fusion.24
  141.1 0.0 copy-done.9
  141.1 3.2 convolution_bitcast_fusion.2
  144.4 29.9 %fusion.27 = bf16[16,72,256]{2,1,0:T(8,128)(2,1)} fusion(bf16[512,16,72]{0,2,1:T(8,128)(2,1)} %bitcast.84, f32[16,256,512]{2,1,0:T(8,128)} %fusion.48, f32[16,256,512]{2,1,0:T(8,128)} %get-tuple-element.47, f32[16,256]{1,0:T(8,128)S(1)} %get-tuple-element.46), kind=kOutput, calls=%fused_computation.35 | convolution fusion | flops 316969472 | bytes 18563072 | tf_op jit(solution)/shard_map/while/body/eval_jaxpr/hqk,khd->qhd/dot_general | solution.py:57
  174.3 4.5 convolution_bitcast_fusion.3
  178.7 189.6 %reduce-scatter.2.cloned.1.call-done = bf16[4,16,1152]{2,1,0:T(8,128)(2,1)} async-done(((bf16[4,512,1152]{2,1,0:T(8,128)(2,1)}), bf16[4,16,1152]{2,1,0:T(8,128)(2,1)}) %reduce-scatter.2.cloned.1.call-update) | async-done | bytes 147472 | tf_op jit(solution)/shard_map/reduce_scatter | solution.py:32
  368.4 0.0 copy-done.8
  368.4 1.9 convolution_bitcast_fusion
  370.3 0.0 copy-done.7
  370.3 0.0 slice-start.1
  370.4 0.9 convolution_bitcast_fusion.1
  371.3 0.0 slice-done
  371.3 0.4 slice-done.1
  371.7 4.6 pad_maximum_fusion
  376.3 27.3 %copy.42 = f32[4,1152,1152]{2,0,1:T(4,128)} copy(f32[4,1152,1152]{2,1,0:T(8,128)S(1)} %pad_maximum_fusion) | data formatting | bytes 42467328 | tf_op jit(solution)/shard_map/stack | solution.py:136
  403.6 0.0 all-reduce.3.cloned.1.call-update
  403.7 1.0 copy-done.2
  404.7 4.1 fusion.35
  408.8 63.4 %psum.7 = f32[1152]{0:T(1024)} all-reduce(f32[1152]{0:T(1024)S(1)} %get-tuple-element.42), channel_id=1, replica_groups=mesh['img'=4,'tile'=32] {'img','tile'}, use_global_device_ids=true, to_apply=%region_8.9 | all-reduce | flops 1152 | bytes 9216 | tf_op jit(solution)/shard_map/psum | solution.py:131
  472.3 2.6 fusion.34
  474.9 0.9 fusion.49
  475.7 1.6 fusion.15
  477.3 149.4 %all-reduce.3.cloned.1.call-done = f32[4,1152,1152]{2,0,1:T(4,128)} async-done(((f32[4,1152,1152]{2,0,1:T(4,128)}), f32[4,1152,1152]{2,0,1:T(4,128)}) %all-reduce.3.cloned.1.call-update) | async-done | bytes 21233680
  626.7 1.6 constant_dynamic-slice_fusion.2
  (11 shorter events, 0.0 us)
Async XLA Ops:
  7.2 45.7 %copy-start = (bf16[1152,1152]{1,0:T(8,128)(2,1)S(1)}, bf16[1152,1152]{1,0:T(8,128)(2,1)}, u32[]{:S(2)}) copy-start(bf16[1152,1152]{1,0:T(8,128)(2,1)} %param.14) | copy-start | bytes 7962628
  9.8 41.2 %all-to-all-start = ((bf16[32,2,16,1152]{3,2,1,0:T(8,128)(2,1)}), bf16[32,2,16,1152]{3,2,1,0:T(8,128)(2,1)}, u32[]{:S(2)}, u32[]{:S(2)}) async-start(bf16[32,2,16,1152]{3,2,1,0:T(8,128)(2,1)} %broadcast_in_dim.27), calls=%async_computation | async-start | bytes 4718592 | tf_op jit(solution)/shard_map/all_to_all | solution.py:18
  20.9 347.5 %reduce-scatter.2.cloned.1.call-start = ((), (), s32[]{:S(2)}) async-start(), calls=%async_computation.2 | async-start | bytes 4866048 | tf_op jit(solution)/shard_map/reduce_scatter | solution.py:32
  21.6 6.0 copy-start.1
  21.6 6.2 copy-start.10
  52.9 3.9 copy-start.6
  81.5 1.7 copy-start.3
  130.0 1.3 copy-start.4
  135.8 490.9 %all-reduce.3.cloned.1.call-start = ((), (), s32[]{:S(2)}) async-start(), calls=%async_computation.3 | async-start | bytes 42467328
  135.8 5.3 copy-start.9
  174.3 194.1 %copy-start.8 = (bf16[2,16,1152]{2,1,0:T(8,128)(2,1)S(1)}, bf16[2,16,1152]{2,1,0:T(8,128)(2,1)}, u32[]{:S(2)}) copy-start(bf16[2,16,1152]{2,1,0:T(8,128)(2,1)} %param.11) | copy-start | bytes 221188
  368.4 1.9 copy-start.7
  368.4 2.9 slice-start
  370.3 1.3 slice-start.1
  403.6 1.1 copy-start.2
  472.2 3.5 copy-start.5
Sparse Core Ops, SparseCore 0:
  135.9 232.4 reduce-scatter.1
  403.8 222.8 all-reduce.2
where the time goes:
time: 637 us; the launch traced here: 635 us
  waiting for transfers between devices  356 us (56%)
  matrix products  123 us (19%)
  blocking collectives  63.4 us (10%)
  local copies, waits for them, and re-layouts  54.4 us (9%)
  between operations  14.9 us (2%)
  other arithmetic  11.7 us (2%)
  starting transfers between devices  11.2 us (2%)
    reduce_scatter x1, waiting for transfers between devices, in_one_piece(): lax.psum_scatter(both, axis, scatter_dimension=dim, tiled=True)  190 us
    unnamed x3, waiting for transfers between devices  149 us
    psum x1, blocking collectives, on_device(): grad_gain = lax.psum(jnp.sum(dh * normed, axis=0), ('img', 'tile'))  63.4 us
    dot_general x1, matrix products, tile_pass(): jnp.einsum('hqk,qhd->khd', dscore, qh, preferred_element_type=jnp.float32)  34.4 us
    dot_general x1, matrix products, tile_pass(): jnp.einsum('hqk,khd->qhd', dscore, kh, preferred_element_type=jnp.float32)  29.9 us
    another operation x1, local copies, waits for them, and re-layouts, on_device(): jnp.stack([jnp.einsum('td,te->de', hidden, dq, preferred_element_type=jnp...  27.3 us
    all_to_all x1, waiting for transfers between devices, copy_for_each(): return lax.all_to_all(copies, axis, split_axis=0, concat_axis=0, tiled=True)  17.4 us
  transfers between devices with their start and end apart: 3, of which 3 were waited for; matrix products, arithmetic and copies ran while one was open for 10% of the time, Pallas kernels for 0%

commit v1 on v0

v1 whole, which is shorter than its diff:
```python
import jax
import jax.numpy as jnp
from jax import lax
from jax.experimental import pallas as pl
from jax.experimental.pallas import tpu as pltpu
from jax.sharding import Mesh, PartitionSpec as P

HEADS = 16
HD = 72
HP = 128
D = 1152
G = 512
F32 = jnp.float32
BF16 = jnp.bfloat16
TILE_AXES = ("x", "yh", "z")
CHIP_AXES = ("yl", "x", "yh", "z")
SWAP = [(0, 1), (1, 0)]


def dot(a, b, ca, cb):
    return lax.dot_general(a, b, (((ca,), (cb,)), ((), ())), preferred_element_type=F32)


def spread_heads_kernel(q_ref, d_ref, qo_ref, do_ref):
    for src, dst in ((q_ref, qo_ref), (d_ref, do_ref)):
        dst[...] = jnp.zeros_like(dst)
        for h in range(HEADS):
            dst[:, h * HP : h * HP + HD] = src[:, h * HD : (h + 1) * HD]


def spread_heads(q, d):
    rows = q.shape[0]
    return pl.pallas_call(
        spread_heads_kernel,
        out_shape=[jax.ShapeDtypeStruct((rows, HEADS * HP), BF16)] * 2,
        name="spread_heads",
    )(q, d)


def spread_weights_kernel(k_ref, v_ref, o_ref):
    o_ref[...] = jnp.zeros_like(o_ref)
    for h in range(HEADS):
        o_ref[:, 2 * h * HP : 2 * h * HP + HD] = k_ref[:, h * HD : (h + 1) * HD]
        o_ref[:, (2 * h + 1) * HP : (2 * h + 1) * HP + HD] = v_ref[:, h * HD : (h + 1) * HD]


def spread_weights(w_key, w_value):
    step = 384
    return pl.pallas_call(
        spread_weights_kernel,
        grid=(D // step,),
        in_specs=[pl.BlockSpec((step, D), lambda i: (i, 0))] * 2,
        out_specs=pl.BlockSpec((step, 2 * HEADS * HP), lambda i: (i, 0)),
        out_shape=jax.ShapeDtypeStruct((D, 2 * HEADS * HP), BF16),
        name="spread_weights",
    )(w_key, w_value)


def attention_kernel(img_ref, g_ref, w_ref, q_ref, d_ref, pay_ref, o_ref, dq_ref, o_scr, dq_scr):
    h = pl.program_id(0)
    scale = HD ** (-0.5)
    guide = g_ref[...].reshape(G, D)
    kv = dot(guide, w_ref[...], 1, 0).astype(BF16)
    k, v = kv[:, :HP], kv[:, HP:]
    q, d = q_ref[...], d_ref[...]
    scores = dot(q, k, 1, 1) * scale
    top = jnp.max(scores, axis=-1, keepdims=True)
    expo = jnp.exp(scores - top)
    probs = expo / jnp.sum(expo, axis=-1, keepdims=True)
    pb = probs.astype(BF16)
    o_scr[h] = dot(pb, v, 1, 0).astype(BF16)
    dprob = dot(d, v, 1, 1)
    delta = jnp.sum(probs * dprob, axis=-1, keepdims=True)
    ds = (probs * (dprob - delta) * scale).astype(BF16)
    dq_scr[h] = dot(ds, k, 1, 0).astype(BF16)
    dk = dot(q, ds, 0, 0)
    dv = dot(d, pb, 0, 0)
    flag = jnp.full((4, G), img_ref[0], jnp.int32).astype(F32)
    for i in range(2):
        for j, part in enumerate((dk, dv)):
            rows = jnp.concatenate([part[36 * i : 36 * i + 36], flag], axis=0)
            pay_ref[i, j] = rows.astype(BF16)

    @pl.when(h == HEADS - 1)
    def _():
        for n in range(HEADS):
            o_ref[:, n * HD : (n + 1) * HD] = o_scr[n][:, :HD]
            dq_ref[:, n * HD : (n + 1) * HD] = dq_scr[n][:, :HD]


def attention(img, whole, w_kv, q, d):
    t = q.shape[0]
    grid_spec = pltpu.PrefetchScalarGridSpec(
        num_scalar_prefetch=1,
        grid=(HEADS,),
        in_specs=[
            pl.BlockSpec((32, pl.Squeezed(), 16, D), lambda h, i: (0, i[0], 0, 0)),
            pl.BlockSpec((D, 2 * HP), lambda h, i: (0, h)),
            pl.BlockSpec((t, HP), lambda h, i: (0, h)),
            pl.BlockSpec((t, HP), lambda h, i: (0, h)),
        ],
        out_specs=[
            pl.BlockSpec((2, 2, 40, G), lambda h, i: (h, 0, 0, 0)),
            pl.BlockSpec((t, D), lambda h, i: (0, 0)),
            pl.BlockSpec((t, D), lambda h, i: (0, 0)),
        ],
        scratch_shapes=[pltpu.VMEM((HEADS, t, HP), BF16), pltpu.VMEM((HEADS, t, HP), BF16)],
    )
    return pl.pallas_call(
        attention_kernel,
        grid_spec=grid_spec,
        out_shape=[
            jax.ShapeDtypeStruct((32, 2, 40, G), BF16),
            jax.ShapeDtypeStruct((t, D), BF16),
            jax.ShapeDtypeStruct((t, D), BF16),
        ],
        name="attention",
    )(img, whole, w_kv, q, d)


def pieces(x, n):
    out = []
    for _ in range(n):
        p = lax.reduce_precision(x, 8, 7)
        out.append(p.astype(BF16))
        x = x - p
    return out


def selection(c):
    j = lax.broadcasted_iota(jnp.int32, (D, 576), 1)
    feature = lax.broadcasted_iota(jnp.int32, (D, 576), 0)
    main = j < 512
    dest = jnp.where(main, j // 8, j - 512)
    row = jnp.where(main, j % 8, 8)
    want = (dest // 32) * 576 + c * 288 + (dest % 32) * 9 + row
    return (feature == want).astype(BF16)


def on_device(tiles, tile_image, guide, gain, w_query, w_key, w_value, w_out, grad_out):
    core = lax.axis_index("c")
    yl = lax.axis_index("yl")
    whole = lax.all_to_all(
        jnp.broadcast_to(guide, (32, *guide.shape)), TILE_AXES, 0, 0, tiled=True
    )
    xf = tiles.astype(F32)
    rstd = lax.rsqrt(jnp.mean(xf * xf, axis=-1, keepdims=True) + 1e-06)
    normed = xf * rstd
    hidden = (normed * gain).astype(BF16)
    query = dot(hidden, w_query, 1, 0).astype(BF16)
    dout = dot(grad_out, w_out, 1, 1).astype(BF16)
    q_wide, d_wide = spread_heads(query, dout)
    w_kv = spread_weights(w_key, w_value)
    pick_mine, pick_theirs = selection(core), selection(1 - core)
    hid_mine = dot(hidden, pick_mine, 1, 0).astype(BF16)
    hid_theirs = dot(hidden, pick_theirs, 1, 0).astype(BF16)
    hid_got = lax.ppermute(hid_theirs, "c", SWAP)
    grad_got = lax.ppermute(grad_out, "c", SWAP)

    pay, outv, dq = attention(tile_image, whole, w_kv, q_wide, d_wide)

    dh = dot(dq, w_query, 1, 1)
    gain_part = jnp.sum(dh * normed, axis=0)
    dn = dh * gain
    grad_tiles = (rstd * (dn - normed * jnp.mean(dn * normed, axis=-1, keepdims=True))).astype(BF16)
    gain_rows = jnp.concatenate([p.reshape(32, 36) for p in pieces(gain_part, 3)], axis=1)
    pay = lax.dynamic_update_slice(pay, gain_rows.reshape(32, 1, 1, 108), (0, 0, 37, 0))
    got = lax.all_to_all(pay, TILE_AXES, 0, 0, tiled=True)

    out_mine = dot(outv, pick_mine, 1, 0).astype(BF16)
    out_theirs = dot(outv, pick_theirs, 1, 0).astype(BF16)
    dq_got = lax.ppermute(dq, "c", SWAP)
    out_got = lax.ppermute(out_theirs, "c", SWAP)
    gq = (dot(hid_mine, dq, 0, 0) + dot(hid_got, dq_got, 0, 0)).astype(BF16)
    go = (dot(out_mine, grad_out, 0, 0) + dot(out_got, grad_got, 0, 0)).astype(BF16)

    flags = got[:, :1, 36:37, :1]
    terms = got[:, :, :36].astype(F32)
    dkv = jnp.stack(
        [jnp.sum(jnp.where(flags == m, terms, 0.0), axis=0) for m in (0, 1)]
    ).astype(BF16)
    gain_mine = jnp.sum(got[:, 0, 37, :108].astype(F32), axis=0).reshape(3, 36).sum(0)
    by_image = whole.transpose(1, 0, 2, 3).reshape(2 * G, D)
    gkv = dot(by_image, dkv.transpose(1, 2, 0, 3).reshape(72, 2 * G), 0, 1)
    gkv = gkv.reshape(2, 2, 288, 72)
    kv_mine = lax.dynamic_index_in_dim(gkv, core, 1, keepdims=False)
    kv_theirs = lax.dynamic_index_in_dim(gkv, 1 - core, 1, keepdims=False)
    kv_sum = (kv_mine + lax.ppermute(kv_theirs, "c", SWAP)).reshape(64, 648)
    gain_mine = gain_mine + lax.ppermute(gain_mine, "c", SWAP)
    tokens = dkv.reshape(144, 32, 16).transpose(1, 0, 2).reshape(1, 32, 2304)
    tokens = jnp.broadcast_to(tokens, (2, 32, 2304)).reshape(64, 2304)
    gains = jnp.broadcast_to(jnp.concatenate(pieces(gain_mine, 3))[None], (64, 108))
    misc = jnp.concatenate(
        [gq[512:], go[512:], *pieces(kv_sum, 2), tokens, gains, jnp.zeros((64, 3204), BF16)],
        axis=1,
    )
    send = jnp.concatenate(
        [gq[:512].reshape(64, 8, D), go[:512].reshape(64, 8, D), misc.reshape(64, 8, D)], axis=1
    )
    recv = lax.all_to_all(send, CHIP_AXES, 0, 0, tiled=True)
    main = jnp.sum(recv[:, :16].astype(F32), axis=0).reshape(2, 8, D)
    rest = recv[:, 16:].reshape(64, 9216)
    ninth = jnp.sum(rest[:, :2304].astype(F32), axis=0).reshape(2, 1, D)
    g_qo = jnp.concatenate([main, ninth], axis=1)
    kv = rest[:, 2304:3600].reshape(2, 32, 2, 9, 2, 36).astype(F32).sum((0, 2))
    g_kv = kv.transpose(2, 1, 0, 3).reshape(2, 9, D)
    grad_weights = jnp.concatenate([g_qo[:1], g_kv, g_qo[1:]], axis=0)
    near = lax.dynamic_index_in_dim(rest.reshape(2, 32, 9216), yl, 0, keepdims=False)
    tok = near[:, 3600:5904].reshape(32, 2, 2, 36, 16)
    tok = tok.transpose(2, 1, 4, 0, 3).reshape(2, 32, D)
    grad_guide = (
        (dot(tok[0], w_key, 1, 1) + dot(tok[1], w_value, 1, 1)).astype(BF16).reshape(guide.shape)
    )
    far = rest.reshape(2, 32, 9216)[:, :, 5904:6012].astype(F32)
    grad_gain = far.reshape(2, 32, 3, 36).sum((0, 2)).reshape(D)
    return (grad_tiles, grad_guide, grad_weights, grad_gain)


def solution(mesh):
    fine = Mesh(mesh.devices.reshape(2, 2, 4, 2, 4), ("yl", "c", "x", "yh", "z"))
    every = ("yl", "c", "x", "yh", "z")
    return jax.shard_map(
        on_device,
        mesh=fine,
        in_specs=(
            P(every, None),
            P(every),
            P(("yl", "c"), TILE_AXES, None),
            P(),
            P(),
            P(),
            P(),
            P(),
            P(every, None),
        ),
        out_specs=(
            P(every, None),
            P(("yl", "c"), TILE_AXES, None),
            P(None, every, None),
            P(),
        ),
        check_vma=False,
    )
```

time: 637 us -> 229 us (0.36)
  waiting for transfers between devices: 356 us -> 68.8 us
  matrix products: 123 us -> 33.9 us
  blocking collectives: 63.4 us -> 0 us
  Pallas kernels: 0 us -> 48.4 us
  local copies, waits for them, and re-layouts: 54.4 us -> 31.3 us
  starting transfers between devices: 11.2 us -> 30.6 us
  between operations: 14.9 us -> 2.1 us
    reduce_scatter x1 -> x0, waiting for transfers between devices: 190 us -> none  [in_one_piece(): lax.psum_scatter(both, axis, scatter_dimension=dim, tiled=True)]
    unnamed x3 -> x0, waiting for transfers between devices: 149 us -> none
    dot_general x16 -> x12, matrix products: 116 us -> 33.9 us  [dot(): lax.dot_general(a, b, (((ca,), (cb,)), ((), ())), preferred_element_type=...]
    psum x1 -> x0, blocking collectives: 63.4 us -> none  [on_device(): grad_gain = lax.psum(jnp.sum(dh * normed, axis=0), ('img', 'tile'))]
    all_to_all x1 -> x3, waiting for transfers between devices: 17.4 us -> 67.8 us  [the longest x1 45.8 us: on_device(): recv = lax.all_to_all(send, CHIP_AXES, 0, 0, tiled=True)]
    pallas_call x0 -> x3, Pallas kernels: none -> 48.4 us  [the longest x1 35.8 us: attention(): pl.pallas_call(attention_kernel, grid_spec=grid_spec, out_shape=[jax.Shap...]
    another operation x3, local copies, waits for them, and re-layouts: 29.1 us -> 2.57 us  [the longest x1 2.45 us: on_device(): rest.reshape(2, 32, 9216)]
    all_to_all x1 -> x3, starting transfers between devices: 11.1 us -> 29.1 us  [the longest x1 11.3 us: on_device(): lax.all_to_all(jnp.broadcast_to(guide, (32, *guide.shape)), TILE_AXES, 0,...]
  transfers between devices with their start and end apart: 3 -> 9, of which waited for: 3 -> 4; matrix products, arithmetic and copies ran while one was open for 10% -> 18% of each run, Pallas kernels for 0% -> 21%
where the time goes in v1:
time: 229 us; the launch traced here: 228 us
  waiting for transfers between devices  68.8 us (30%)
  Pallas kernels  48.4 us (21%)
  matrix products  33.9 us (15%)
  local copies, waits for them, and re-layouts  31.3 us (14%)
  starting transfers between devices  30.6 us (13%)
  other arithmetic  12.5 us (5%)
    all_to_all x1, waiting for transfers between devices, on_device(): recv = lax.all_to_all(send, CHIP_AXES, 0, 0, tiled=True)  45.8 us
    pallas_call x1, Pallas kernels, attention(): pl.pallas_call(attention_kernel, grid_spec=grid_spec, out_shape=[jax.Shap...  35.8 us
    dot_general x12, matrix products, dot(): lax.dot_general(a, b, (((ca,), (cb,)), ((), ())), preferred_element_type=...  33.9 us
    all_to_all x1, waiting for transfers between devices, on_device(): got = lax.all_to_all(pay, TILE_AXES, 0, 0, tiled=True)  13.9 us
    all_to_all x1, starting transfers between devices, on_device(): lax.all_to_all(jnp.broadcast_to(guide, (32, *guide.shape)), TILE_AXES, 0,...  11.3 us
    all_to_all x1, starting transfers between devices, on_device(): recv = lax.all_to_all(send, CHIP_AXES, 0, 0, tiled=True)  9.47 us
    pallas_call x1, Pallas kernels, spread_weights(): pl.pallas_call(spread_weights_kernel, grid=(D // step,), in_specs=[pl.Blo...  9.2 us
    all_to_all x1, starting transfers between devices, on_device(): got = lax.all_to_all(pay, TILE_AXES, 0, 0, tiled=True)  8.32 us
  transfers between devices with their start and end apart: 9, of which 4 were waited for; matrix products, arithmetic and copies ran while one was open for 18% of the time, Pallas kernels for 21%

profile of v1, /device:TPU:2, one launch (start us, length us, event | category | flops | bytes accessed | tf_op | source)
XLA Modules:
  0.0 227.6 jit_solution(4600087237603761580)
XLA Ops:
  0.6 2.6 %broadcast_in_dim.48 = bf16[32,2,16,1152]{3,2,1,0:T(8,128)(2,1)} broadcast(bf16[2,16,1152]{2,1,0:T(8,128)(2,1)} %param.11), dimensions={1,2,3} | broadcast | bytes 2433024 | tf_op jit(solution)/shard_map/broadcast_in_dim | solution.py:144
  3.2 11.3 %all-to-all-start = ((bf16[32,2,16,1152]{3,2,1,0:T(8,128)(2,1)}), bf16[32,2,16,1152]{3,2,1,0:T(8,128)(2,1)}, u32[]{:S(2)}, u32[]{:S(2)}) async-start(bf16[32,2,16,1152]{3,2,1,0:T(8,128)(2,1)} %broadcast_in_dim.48), calls=%async_computation | async-start | bytes 4718592 | tf_op jit(solution)/shard_map/all_to_all | solution.py:143
  14.9 0.2 copy-done.31
  15.3 1.8 convolution_convert_fusion.4
  17.0 0.5 collective-permute-start.3
  18.2 3.8 %convolution_convert_fusion.d_ref = bf16[256,1152]{1,0:T(8,128)(2,1)} fusion(bf16[256,1152]{1,0:T(8,128)(2,1)} %param.17, bf16[1152,1152]{1,0:T(8,128)(2,1)} %param.16), kind=kOutput, calls=%fused_computation.25 | convolution fusion | flops 679772160 | bytes 3833856 | tf_op jit(solution)/shard_map/dot_general | solution.py:21
  22.0 1.9 convolution_convert_fusion.1.q_ref
  23.9 3.4 %spread_heads.1 = (bf16[256,2048]{1,0:T(8,128)(2,1)}, bf16[256,2048]{1,0:T(8,128)(2,1)}) custom-call(bf16[256,1152]{1,0:T(8,128)(2,1)} %convolution_convert_fusion.1.q_ref, bf16[256,1152]{1,0:T(8,128)(2,1)} %convolution_convert_fusion.d_ref), custom_call_target="tpu_custom_call" | custom-call | tf_op jit(solution)/shard_map/spread_heads/pallas_call | solution.py:33
  27.3 9.2 %spread_weights.1.w_ref = bf16[1152,4096]{1,0:T(8,128)(2,1)} custom-call(bf16[1152,1152]{1,0:T(8,128)(2,1)} %k_ref.1, bf16[1152,1152]{1,0:T(8,128)(2,1)} %v_ref.1), custom_call_target="tpu_custom_call" | custom-call | tf_op jit(solution)/shard_map/spread_weights/pallas_call | solution.py:49
  36.5 8.1 %all-to-all-done.g_ref = bf16[32,2,16,1152]{3,2,1,0:T(8,128)(2,1)} async-done(((bf16[32,2,16,1152]{3,2,1,0:T(8,128)(2,1)}), bf16[32,2,16,1152]{3,2,1,0:T(8,128)(2,1)}, u32[]{:S(2)}, u32[]{:S(2)}) %all-to-all-start) | async-done | bytes 2359328 | tf_op jit(solution)/shard_map/all_to_all | solution.py:143
  44.6 35.8 %attention.1 = (bf16[32,2,40,512]{3,2,1,0:T(8,128)(2,1)}, bf16[256,1152]{1,0:T(8,128)(2,1)}, bf16[256,1152]{1,0:T(8,128)(2,1)}) custom-call(s32[1]{0:T(128)S(6)} %copy.55.img_ref, bf16[32,2,16,1152]{3,2,1,0:T(8,128)(2,1)} %all-to-all-done.g_ref, bf16[1152,4096]{1,0:T(8,128)(2,1)} %spread_weights.1.w_ref, bf16[256,2048]{1,0:T(8,128)(2,1)} %get-tuple-element.9.q_ref, ...), custom_call_target="tpu_custom_call" | custom-call | tf_op jit(solution)/shard_map/attention/pallas_call | solution.py:109
  80.4 3.7 %fusion.19 = (f32[1152]{0:T(1024)S(1)}, f32[256]{0:T(256)}, f32[256,1152]{1,0:T(8,128)}) fusion(bf16[256,1152]{1,0:T(8,128)(2,1)S(1)} %copy-done.8, f32[256]{0:T(256)} %copy-done.12, f32[1152]{0:T(1024)S(1)} %copy-done.11, bf16[256,1152]{1,0:T(8,128)(2,1)} %get-tuple-element.11, bf16[1152,1152]{1,0:T(8,128)(2,1)S(1)} %copy-done), kind=kOutput, calls=%fused_computation.45 | convolution fusion | flops 681540224 | bytes 5024768 | tf_op jit(solution)/shard_map/dot_general | solution.py:21
  84.5 1.9 dynamic_update_slice.3
  86.4 8.3 %all-to-all-start.1 = ((bf16[32,2,40,512]{3,2,1,0:T(8,128)(2,1)}), bf16[32,2,40,512]{3,2,1,0:T(8,128)(2,1)S(1)}, u32[]{:S(2)}, u32[]{:S(2)}) async-start(bf16[32,2,40,512]{3,2,1,0:T(8,128)(2,1)} %dynamic_update_slice.3), calls=%async_computation.1 | async-start | bytes 5242880 | tf_op jit(solution)/shard_map/all_to_all | solution.py:168
  94.8 4.4 %fusion.21 = f32[576,1152]{1,0:T(8,128)} fusion(bf16[256,1152]{1,0:T(8,128)(2,1)} %get-tuple-element.11, bf16[256,1152]{1,0:T(8,128)(2,1)S(1)} %copy-done.8, f32[1152]{0:T(1024)S(1)} %copy-done.11, f32[256]{0:T(256)S(1)} %copy-done.13, s32[576]{0:T(1024)S(1)} %copy-done.25, s32[576]{0:T(1024)S(1)} %copy-done.28, s32[]{:T(128)S(6)} %mul.74, ...), kind=kOutput, calls=%fused_computation.49 | convolution fusion | flops 700047360 | bytes 3852740 | tf_op jit(solution)/shard_map/dot_general | solution.py:21
  99.3 2.0 convolution_convert_fusion.2
  101.5 4.6 %fusion.22 = f32[576,1152]{1,0:T(8,128)} fusion(bf16[256,1152]{1,0:T(8,128)(2,1)} %param.17, bf16[256,1152]{1,0:T(8,128)(2,1)} %get-tuple-element.12, s32[576]{0:T(1024)S(1)} %copy-done.26, s32[576]{0:T(1024)S(1)} %copy-done.29, s32[]{:T(128)S(6)} %mul.74, pred[576]{0:T(1024)(128)(4,1)S(1)} %copy-done.36, pred[576]{0:T(1024)(128)(4,1)S(1)} %copy-done.33, ...), kind=kOutput, calls=%fused_computation.50 | convolution fusion | flops 698867712 | bytes 3847108 | tf_op jit(solution)/shard_map/dot_general | solution.py:21
  106.0 3.4 %copy.30 = bf16[2,32,16,1152]{3,2,1,0:T(8,128)(2,1)} copy(bf16[2,32,16,1152]{3,2,0,1:T(8,128)(2,1)} %bitcast.6) | data formatting | bytes 4718592 | tf_op jit(solution)/shard_map/transpose | solution.py:183
  109.5 1.8 fusion.3
  111.2 1.2 slice_bitcast_fusion
  112.5 1.6 fusion.2
  114.2 1.1 slice_bitcast_fusion.1
  115.3 13.9 %all-to-all-done.1 = bf16[32,2,40,512]{3,2,1,0:T(8,128)(2,1)S(1)} async-done(((bf16[32,2,40,512]{3,2,1,0:T(8,128)(2,1)}), bf16[32,2,40,512]{3,2,1,0:T(8,128)(2,1)S(1)}, u32[]{:S(2)}, u32[]{:S(2)}) %all-to-all-start.1) | async-done | bytes 2621472 | tf_op jit(solution)/shard_map/all_to_all | solution.py:168
  129.2 1.2 compare_reduce_fusion.1
  130.4 1.3 fusion
  131.9 0.2 maximum_convert_fusion
  132.1 0.2 fusion.63
  132.5 0.5 copy.34
  133.0 0.3 convert_element_type.112
  133.3 0.6 copy.35
  134.0 0.2 copy.36
  134.4 2.2 convolution_bitcast_fusion
  136.6 0.4 reshape.100
  137.0 0.4 constant_dynamic-slice_fusion.2
  137.4 0.8 collective-permute-start.4
  138.3 1.0 collective-permute-done.4
  139.6 0.7 fusion.25
  140.4 3.0 %concatenate.20 = bf16[64,9216]{1,0:T(8,128)(2,1)} concatenate(bf16[64,1152]{1,0:T(8,128)(2,1)S(1)} %slice.72, bf16[64,1152]{1,0:T(8,128)(2,1)S(1)} %slice-done, bf16[64,648]{1,0:T(8,128)(2,1)} %get-tuple-element.25, bf16[64,648]{1,0:T(8,128)(2,1)S(1)} %get-tuple-element.24, bf16[64,2304]{1,0:T(8,128)(2,1)S(1)} %bitcast.77, bf16[64,108]{1,0:T(8,128)(2,1)S(1)} %broadcast_in_dim.56, ...), dimensions={1} | concatenate | bytes 2359296 | tf_op jit(solution)/shard_map/concatenate | solution.py:193
  143.4 1.4 copy.47
  144.8 1.9 pad_maximum_fusion
  146.8 9.5 %all-to-all-start.2 = ((bf16[64,24,1152]{2,1,0:T(8,128)(2,1)}), bf16[64,24,1152]{2,1,0:T(8,128)(2,1)S(1)}, u32[]{:S(2)}, u32[]{:S(2)}) async-start(bf16[64,24,1152]{2,1,0:T(8,128)(2,1)} %pad_maximum_fusion), calls=%async_computation.2 | async-start | bytes 7077888 | tf_op jit(solution)/shard_map/all_to_all | solution.py:200
  156.3 2.6 %fusion.18 = bf16[256,1152]{1,0:T(8,128)(2,1)} fusion(bf16[256,1152]{1,0:T(8,128)(2,1)} %param.9, f32[256,1152]{1,0:T(8,128)} %get-tuple-element.34, f32[256]{0:T(256)S(1)} %broadcast_multiply_fusion, f32[1152]{0:T(1024)S(1)} %copy-done.11, f32[256]{0:T(256)S(1)} %copy-done.14), kind=kLoop, calls=%fused_computation.44 | loop fusion | flops 2064384 | bytes 2365952 | tf_op jit(solution)/shard_map/convert_element_type | solution.py:165
  158.9 45.8 %all-to-all-done.2 = bf16[64,24,1152]{2,1,0:T(8,128)(2,1)S(1)} async-done(((bf16[64,24,1152]{2,1,0:T(8,128)(2,1)}), bf16[64,24,1152]{2,1,0:T(8,128)(2,1)S(1)}, u32[]{:S(2)}, u32[]{:S(2)}) %all-to-all-start.2) | async-done | bytes 3538976 | tf_op jit(solution)/shard_map/all_to_all | solution.py:200
  204.6 1.1 slice.77
  205.7 1.5 copy.48
  207.2 0.8 slice_convert_fusion
  208.0 2.4 %reshape_reshape.4 = bf16[2,32,9216]{2,1,0:T(8,128)(2,1)} reshape(bf16[64,8,1152]{2,1,0:T(8,128)(2,1)} %slice.77) | data formatting | bytes 2359296 | tf_op jit(solution)/shard_map/reshape;reshape | solution.py:208
  210.5 0.6 reshape.109
  211.1 0.3 convert_reduce_fusion
  211.4 0.8 fusion.26
  212.2 0.7 copy.41
  212.9 0.7 copy.42
  213.6 2.1 reshape.112
  215.6 1.0 reduce_sum.118
  216.6 0.3 reshape.110
  217.0 1.1 copy.45
  218.4 0.4 copy.38
  218.7 0.4 squeeze.21
  219.1 2.8 %fusion.43 = f32[32,1152]{1,0:T(8,128)S(1)} fusion(bf16[32,1152]{1,0:T(8,128)(2,1)S(1)} %squeeze.21, bf16[1152,1152]{1,0:T(8,128)(2,1)} %k_ref.1), kind=kOutput, calls=%fused_computation.103 | convolution fusion | flops 84934656 | bytes 2875392 | tf_op jit(solution)/shard_map/dot_general | solution.py:21
  221.9 0.4 copy.39
  222.3 0.4 squeeze.22
  222.8 0.7 reshape.111
  223.5 3.3 %fusion.9 = bf16[32,1152]{1,0:T(8,128)(2,1)} fusion(f32[32,1152]{1,0:T(8,128)S(1)} %fusion.43, bf16[32,1152]{1,0:T(8,128)(2,1)S(1)} %squeeze.22, bf16[1152,1152]{1,0:T(8,128)(2,1)} %v_ref.1), kind=kOutput, calls=%fused_computation.29 | convolution fusion | flops 85008384 | bytes 2949120 | tf_op jit(solution)/shard_map/dot_general | solution.py:21
  226.8 0.8 pad_maximum_fusion.1
  (125 shorter events, 2.4 us)
Async XLA Ops:
  0.6 21.4 %copy-start = (bf16[1152,1152]{1,0:T(8,128)(2,1)S(1)}, bf16[1152,1152]{1,0:T(8,128)(2,1)}, u32[]{:S(2)}) copy-start(bf16[1152,1152]{1,0:T(8,128)(2,1)} %param.13) | copy-start | bytes 7962628
  3.2 11.4 %copy-start.8 = (bf16[256,1152]{1,0:T(8,128)(2,1)S(1)}, bf16[256,1152]{1,0:T(8,128)(2,1)}, u32[]{:S(2)}) copy-start(bf16[256,1152]{1,0:T(8,128)(2,1)} %param.9) | copy-start | bytes 1769476
  3.2 12.0 %copy-start.11 = (f32[1152]{0:T(1024)S(1)}, f32[1152]{0:T(1024)}, u32[]{:S(2)}) copy-start(f32[1152]{0:T(1024)} %param.12) | copy-start | bytes 13828
  3.2 41.4 %all-to-all-start = ((bf16[32,2,16,1152]{3,2,1,0:T(8,128)(2,1)}), bf16[32,2,16,1152]{3,2,1,0:T(8,128)(2,1)}, u32[]{:S(2)}, u32[]{:S(2)}) async-start(bf16[32,2,16,1152]{3,2,1,0:T(8,128)(2,1)} %broadcast_in_dim.48), calls=%async_computation | async-start | bytes 4718592 | tf_op jit(solution)/shard_map/all_to_all | solution.py:143
  14.5 0.6 copy-start.31
  14.6 0.6 copy-start.34
  14.6 0.6 copy-start.37
  14.6 0.6 copy-start.15
  14.6 0.6 copy-start.18
  14.6 0.6 copy-start.21
  14.7 0.6 copy-start.24
  14.7 0.6 copy-start.27
  14.9 7.1 %copy-start.12 = (f32[256]{0:T(256)}, f32[256]{0:T(256)S(1)}, u32[]{:S(2)}) copy-start(f32[256]{0:T(256)S(1)} %add_rsqrt_fusion) | copy-start | bytes 3076
  17.0 95.5 %collective-permute-start = (bf16[256,576]{0,1:T(8,128)(2,1)}, bf16[256,576]{0,1:T(8,128)(2,1)S(1)}, u32[]{:S(2)}, u32[]{:S(2)}) collective-permute-start(bf16[256,576]{0,1:T(8,128)(2,1)} %convolution_convert_fusion.4), channel_id=1, source_target_pairs={{0,32},{32,0},{1,33},{33,1},{2,34},{34,2},{3,35},{35,3},{4,36},{36... | collective-permute-start | bytes 884744 | tf_op jit(solution)/shard_map/ppermute | solution.py:157
  17.0 92.4 %collective-permute-start.3 = (bf16[256,1152]{1,0:T(8,128)(2,1)}, bf16[256,1152]{1,0:T(8,128)(2,1)}, u32[]{:S(2)}, u32[]{:S(2)}) collective-permute-start(bf16[256,1152]{1,0:T(8,128)(2,1)} %param.17), channel_id=1, source_target_pairs={{0,32},{32,0},{1,33},{33,1},{2,34},{34,2},{3,35},{35,3},{4,36},{36... | collective-permute-start | bytes 1769480 | tf_op jit(solution)/shard_map/ppermute | solution.py:158
  84.1 10.6 %copy-start.13 = (f32[256]{0:T(256)S(1)}, f32[256]{0:T(256)}, u32[]{:S(2)}) copy-start(f32[256]{0:T(256)} %copy-done.12) | copy-start | bytes 3076
  84.1 10.6 %copy-start.16 = (s32[576]{0:T(1024)S(1)}, s32[576]{0:T(1024)}, u32[]{:S(2)}) copy-start(s32[576]{0:T(1024)} %copy-done.15) | copy-start | bytes 6916
  84.1 10.6 %copy-start.19 = (s32[576]{0:T(1024)S(1)}, s32[576]{0:T(1024)}, u32[]{:S(2)}) copy-start(s32[576]{0:T(1024)} %copy-done.18) | copy-start | bytes 6916
  84.1 10.6 %copy-start.22 = (s32[576]{0:T(1024)S(1)}, s32[576]{0:T(1024)}, u32[]{:S(2)}) copy-start(s32[576]{0:T(1024)} %copy-done.21) | copy-start | bytes 6916
  84.1 10.6 %copy-start.25 = (s32[576]{0:T(1024)S(1)}, s32[576]{0:T(1024)}, u32[]{:S(2)}) copy-start(s32[576]{0:T(1024)} %copy-done.24) | copy-start | bytes 6916
  84.1 10.6 %copy-start.28 = (s32[576]{0:T(1024)S(1)}, s32[576]{0:T(1024)}, u32[]{:S(2)}) copy-start(s32[576]{0:T(1024)} %copy-done.27) | copy-start | bytes 6916
  84.1 10.6 %copy-start.32 = (pred[576]{0:T(1024)(128)(4,1)S(1)}, pred[576]{0:T(1024)(128)(4,1)}, u32[]{:S(2)}) copy-start(pred[576]{0:T(1024)(128)(4,1)} %copy-done.31) | copy-start | bytes 1732
  84.2 10.6 %copy-start.35 = (pred[576]{0:T(1024)(128)(4,1)S(1)}, pred[576]{0:T(1024)(128)(4,1)}, u32[]{:S(2)}) copy-start(pred[576]{0:T(1024)(128)(4,1)} %copy-done.34) | copy-start | bytes 1732
  84.2 28.3 %collective-permute-start.1 = (bf16[256,1152]{1,0:T(8,128)(2,1)}, bf16[256,1152]{1,0:T(8,128)(2,1)}, u32[]{:S(2)}, u32[]{:S(2)}) collective-permute-start(bf16[256,1152]{1,0:T(8,128)(2,1)} %get-tuple-element.11), channel_id=1, source_target_pairs={{0,32},{32,0},{1,33},{33,1},{2,34},{34,2},{3,35},{35,3},{4,36},{36... | collective-permute-start | bytes 1769480 | tf_op jit(solution)/shard_map/ppermute | solution.py:172
  86.4 42.8 %all-to-all-start.1 = ((bf16[32,2,40,512]{3,2,1,0:T(8,128)(2,1)}), bf16[32,2,40,512]{3,2,1,0:T(8,128)(2,1)S(1)}, u32[]{:S(2)}, u32[]{:S(2)}) async-start(bf16[32,2,40,512]{3,2,1,0:T(8,128)(2,1)} %dynamic_update_slice.3), calls=%async_computation.1 | async-start | bytes 5242880 | tf_op jit(solution)/shard_map/all_to_all | solution.py:168
  94.8 4.4 %copy-start.38 = (pred[576]{0:T(1024)(128)(4,1)S(1)}, pred[576]{0:T(1024)(128)(4,1)}, u32[]{:S(2)}) copy-start(pred[576]{0:T(1024)(128)(4,1)} %copy-done.37) | copy-start | bytes 1732
  99.2 2.2 copy-start.17
  99.2 2.2 copy-start.20
  99.2 2.2 copy-start.23
  99.2 2.2 copy-start.26
  99.2 2.2 copy-start.29
  99.2 2.2 copy-start.33
  99.2 2.2 copy-start.36
  101.3 8.1 %collective-permute-start.2 = (bf16[256,576]{0,1:T(8,128)(2,1)S(1)}, bf16[256,576]{0,1:T(8,128)(2,1)S(1)}, u32[]{:S(2)}, u32[]{:S(2)}) collective-permute-start(bf16[256,576]{0,1:T(8,128)(2,1)S(1)} %convolution_convert_fusion.2), channel_id=1, source_target_pairs={{0,32},{32,0},{1,33},{33,1},{2,34},{34,2},{3,35},{35,3},{4,36},{36... | collective-permute-start | bytes 884744 | tf_op jit(solution)/shard_map/ppermute | solution.py:173
  106.0 3.4 %copy-start.7 = (f32[576,1152]{1,0:T(8,128)S(1)}, f32[576,1152]{1,0:T(8,128)}, u32[]{:S(2)}) copy-start(f32[576,1152]{1,0:T(8,128)} %fusion.22) | copy-start | bytes 7962628
  109.4 3.1 %copy-start.6 = (f32[576,1152]{1,0:T(8,128)S(1)}, f32[576,1152]{1,0:T(8,128)}, u32[]{:S(2)}) copy-start(f32[576,1152]{1,0:T(8,128)} %fusion.21) | copy-start | bytes 7962628
  111.2 2.9 %copy-start.2 = (bf16[576,1152]{1,0:T(8,128)(2,1)}, bf16[576,1152]{1,0:T(8,128)(2,1)S(1)}, u32[]{:S(2)}) copy-start(bf16[576,1152]{1,0:T(8,128)(2,1)S(1)} %fusion.3) | copy-start | bytes 3981316
  132.5 5.7 %collective-permute-start.5 = (f32[36]{0:T(128)S(1)}, f32[36]{0:T(128)S(1)}, u32[]{:S(2)}, u32[]{:S(2)}) collective-permute-start(f32[36]{0:T(128)S(1)} %reduce_sum.115), channel_id=1, source_target_pairs={{0,32},{32,0},{1,33},{33,1},{2,34},{34,2},{3,35},{35,3},{4,36},{36... | collective-permute-start | bytes 440 | tf_op jit(solution)/shard_map/ppermute | solution.py:189
  136.6 3.8 %slice-start = ((bf16[576,1152]{1,0:T(8,128)(2,1)}), bf16[64,1152]{1,0:T(8,128)(2,1)S(1)}, s32[]{:S(2)}) async-start(bf16[576,1152]{1,0:T(8,128)(2,1)} %copy-done.2), calls=%async_computation.3 | async-start | bytes 294912 | tf_op jit(solution)/shard_map/slice | solution.py:194
  137.4 1.9 collective-permute-start.4
  139.6 5.2 %copy-start.3 = (bf16[64,8,1152]{2,1,0:T(8,128)(2,1)S(1)}, bf16[64,8,1152]{2,1,0:T(8,128)(2,1)}, u32[]{:S(2)}) copy-start(bf16[64,8,1152]{2,1,0:T(8,128)(2,1)} %slice_bitcast_fusion) | copy-start | bytes 3538948
  139.6 5.2 %copy-start.4 = (bf16[64,8,1152]{2,1,0:T(8,128)(2,1)S(1)}, bf16[64,8,1152]{2,1,0:T(8,128)(2,1)}, u32[]{:S(2)}) copy-start(bf16[64,8,1152]{2,1,0:T(8,128)(2,1)} %slice_bitcast_fusion.1) | copy-start | bytes 3538948
  146.8 9.5 %copy-start.30 = (f32[256]{0:T(256)S(1)}, f32[256]{0:T(256)}, u32[]{:S(2)}) copy-start(f32[256]{0:T(256)} %get-tuple-element.19) | copy-start | bytes 3076
  146.8 9.5 %copy-start.14 = (f32[256]{0:T(256)S(1)}, f32[256]{0:T(256)}, u32[]{:S(2)}) copy-start(f32[256]{0:T(256)} %copy-done.12) | copy-start | bytes 3076
  146.8 57.8 %all-to-all-start.2 = ((bf16[64,24,1152]{2,1,0:T(8,128)(2,1)}), bf16[64,24,1152]{2,1,0:T(8,128)(2,1)S(1)}, u32[]{:S(2)}, u32[]{:S(2)}) async-start(bf16[64,24,1152]{2,1,0:T(8,128)(2,1)} %pad_maximum_fusion), calls=%async_computation.2 | async-start | bytes 7077888 | tf_op jit(solution)/shard_map/all_to_all | solution.py:200
  211.4 5.5 %copy-start.5 = (bf16[2,32,9216]{2,1,0:T(8,128)(2,1)S(1)}, bf16[2,32,9216]{2,1,0:T(8,128)(2,1)}, u32[]{:S(2)}) copy-start(bf16[2,32,9216]{2,1,0:T(8,128)(2,1)} %reshape_reshape.4) | copy-start | bytes 3538948
  218.7 8.9 %copy-start.1 = (bf16[1152,1152]{1,0:T(8,128)(2,1)S(1)}, bf16[1152,1152]{1,0:T(8,128)(2,1)}, u32[]{:S(2)}) copy-start(bf16[1152,1152]{1,0:T(8,128)(2,1)} %param.13) | copy-start | bytes 7962628
  221.9 4.9 %copy-start.9 = (f32[1,9,1152]{2,0,1:T(1,128)S(1)}, f32[1,9,1152]{2,0,1:T(1,128)}, u32[]{:S(2)}) copy-start(f32[1,9,1152]{2,0,1:T(1,128)} %copy.41) | copy-start | bytes 124420
  221.9 4.9 %copy-start.10 = (f32[1,9,1152]{2,0,1:T(1,128)S(1)}, f32[1,9,1152]{2,0,1:T(1,128)}, u32[]{:S(2)}) copy-start(f32[1,9,1152]{2,0,1:T(1,128)} %copy.42) | copy-start | bytes 124420
